TPU v7x, 32 devices: a whole 2x2x4 slice. The times are simulated.
32 devices in a mesh: seq: 16 (over z, y, x), grp: 2 (over core).
Axes of the slice: x: 2, y: 2, z: 4, core: 2. Of those that a mesh axis runs over, the one named last changes fastest.
Arguments:
- key_rows: bfloat16 [32768, 4096], P('seq', 'grp')
- probe_ints: int32 [4096, 512], P('grp'), may hold values from -2 to 2
- rank_keep: int32 [1], replicated, may hold values from 128 to 511
Outputs:
- latents: float32 [32768, 512], P('seq', 'grp')
- latent_basis: float32 [512, 4096], P('seq', 'grp')
All inputs are finite; a program needn't handle non-finite values.
Results may differ from a plain program's by a relative error of at most 0.00098.
Values may be sent and summed in bfloat16 or wider, within the bound.
A program may use at most 128 MiB of HBM per device.

v0:
```python
import math
import jax
import jax.numpy as jnp
from jax import lax
from jax.sharding import PartitionSpec as P


def on_device(key_rows, probe_ints, rank_keep):
    seq_count = lax.axis_size("seq")
    tokens = key_rows.shape[0] * seq_count
    root_tokens = math.sqrt(tokens)
    probes = (probe_ints.astype(jnp.float32) * 0.015625).astype(jnp.bfloat16)
    whole_keys = lax.all_gather(key_rows, "grp", axis=1, tiled=True)
    whole_probes = lax.all_gather(probes, "grp", axis=0, tiled=True)
    sketch = jnp.dot(whole_keys, whole_probes, preferred_element_type=jnp.float32)
    contract = (((0,), (0,)), ((), ()))
    local_gram = lax.dot_general(sketch, sketch, contract, precision=lax.Precision.HIGHEST)
    gram_matrix = lax.psum(local_gram, "seq")
    lower_factor = jnp.linalg.cholesky(gram_matrix)
    identity = jnp.eye(gram_matrix.shape[0], dtype=jnp.float32)
    inverse = lax.linalg.triangular_solve(lower_factor, identity, left_side=True, lower=True)
    orthonormal = jnp.dot(sketch, inverse.T, precision=lax.Precision.HIGHEST) * root_tokens
    probe_count = orthonormal.shape[1]
    part_width = probe_count // lax.axis_size("grp")
    first_column = lax.axis_index("grp") * part_width
    columns = first_column + jnp.arange(part_width)
    own_columns = lax.dynamic_slice_in_dim(orthonormal, first_column, part_width, 1)
    latents = jnp.where(columns[None, :] < rank_keep[0], own_columns, jnp.float32(0.0))
    rounded = orthonormal.astype(jnp.bfloat16)
    rows_out = probe_count // seq_count
    summed = lax.psum_scatter(
        lax.dot_general(rounded, key_rows, contract, preferred_element_type=jnp.float32),
        "seq",
        scatter_dimension=0,
        tiled=True,
    )
    row_index = lax.axis_index("seq") * rows_out + jnp.arange(rows_out)
    latent_basis = jnp.where(
        row_index[:, None] < rank_keep[0], summed / root_tokens, jnp.float32(0.0)
    )
    return (latents, latent_basis)


def solution(mesh):
    in_specs = (P("seq", "grp"), P("grp", None), P())
    out_specs = (P("seq", "grp"), P("seq", "grp"))
    return jax.shard_map(
        on_device, mesh=mesh, in_specs=in_specs, out_specs=out_specs, check_vma=False
    )
```

profile of v0, /device:TPU:0, one launch (start us, length us, event | category | flops | bytes accessed | tf_op | source)
XLA Modules:
  0.0 463.2 jit_solution(5321967595677841850)
XLA Ops:
  7.2 4.1 multiply_convert_fusion
  11.4 0.7 all-gather.5.cloned.1.call-update
  12.1 15.7 %all-gather.3.cloned.1.call-done = bf16[4096,512]{1,0:T(8,128)(2,1)} async-done(((bf16[2048,512]{1,0:T(8,128)(2,1)}), bf16[4096,512]{1,0:T(8,128)(2,1)}) %all-gather.3.cloned.1.call-update) | async-done | bytes 4194320 | tf_op jit(solution)/shard_map/all_gather | solution.py:14
  27.8 32.8 %all-gather.5.cloned.1.call-done = bf16[2048,4096]{1,0:T(8,128)(2,1)} async-done(((bf16[2048,2048]{1,0:T(8,128)(2,1)}), bf16[2048,4096]{1,0:T(8,128)(2,1)}) %all-gather.5.cloned.1.call-update) | async-done | bytes 16777232 | tf_op jit(solution)/shard_map/all_gather | solution.py:13
  60.7 13.0 %fusion.42 = f32[512,2048]{1,0:T(8,128)S(1)} fusion(bf16[4096,512]{1,0:T(8,128)(2,1)} %all-gather.3.cloned.1.call-done, bf16[2048,4096]{1,0:T(8,128)(2,1)} %all-gather.5.cloned.1.call-done), kind=kOutput, calls=%fused_computation.84 | convolution fusion | flops 8589934592 | bytes 25165824 | tf_op jit(solution)/shard_map/dot_general | solution.py:15
  73.7 1.9 copy-done
  75.7 7.7 %fusion.43 = f32[512,512]{0,1:T(8,128)} fusion(f32[512,2048]{1,0:T(8,128)S(1)} %fusion.42), kind=kOutput, calls=%fused_computation.85 | convolution fusion | flops 6442450944 | bytes 5242880 | tf_op jit(solution)/shard_map/dot_general | solution.py:17
  83.6 0.8 iota_compare_fusion
  84.5 111.9 %all-reduce.3.cloned.1.call-done = f32[512,512]{0,1:T(8,128)} async-done(((f32[512,512]{0,1:T(8,128)}), f32[512,512]{0,1:T(8,128)}) %all-reduce.3.cloned.1.call-update) | async-done | bytes 1048592 | tf_op jit(solution)/shard_map/psum | solution.py:18
  196.4 1.6 copy.6
  198.0 1.4 fusion.9
  199.5 11.7 %cholesky.104 = f32[128,128]{1,0:T(8,128)S(1)} custom-call(f32[128,128]{1,0:T(8,128)S(1)} %cholesky.266), custom_call_target="Cholesky" | custom-call | tf_op jit(solution)/shard_map/jit(cholesky)/cholesky | solution.py:19
  211.2 9.8 %custom-call.30 = f32[1,128,128]{1,2,0:T(8,128)S(1)} custom-call(f32[1,128,128]{2,1,0:T(8,128)S(1)} %get-tuple-element.29), custom_call_target="InvertDiagBlocksLowerTriangular" | custom-call | tf_op jit(solution)/shard_map/jit(cholesky)/cholesky | solution.py:19
  221.2 0.3 constant_dynamic-update-slice_fusion.2
  221.5 0.3 convolution_subtract_fusion.3
  221.8 11.7 %cholesky.217 = f32[128,128]{1,0:T(8,128)S(1)} custom-call(f32[128,128]{1,0:T(8,128)S(1)} %cholesky.270), custom_call_target="Cholesky" | custom-call | tf_op jit(solution)/shard_map/jit(cholesky)/cholesky | solution.py:19
  233.6 10.2 %custom-call.31 = f32[1,128,128]{1,2,0:T(8,128)S(1)} custom-call(f32[1,128,128]{2,1,0:T(8,128)S(1)} %get-tuple-element.26), custom_call_target="InvertDiagBlocksLowerTriangular" | custom-call | tf_op jit(solution)/shard_map/jit(cholesky)/cholesky | solution.py:19
  244.0 0.4 convolution_subtract_fusion.4
  244.4 11.7 %cholesky.238 = f32[128,128]{1,0:T(8,128)S(1)} custom-call(f32[128,128]{1,0:T(8,128)S(1)} %cholesky.275), custom_call_target="Cholesky" | custom-call | tf_op jit(solution)/shard_map/jit(cholesky)/cholesky | solution.py:19
  256.2 0.7 compare_reduce_fusion.1
  256.8 9.8 %custom-call.32 = f32[1,128,128]{1,2,0:T(8,128)S(1)} custom-call(f32[1,128,128]{2,1,0:T(8,128)S(1)} %get-tuple-element.23), custom_call_target="InvertDiagBlocksLowerTriangular" | custom-call | tf_op jit(solution)/shard_map/jit(cholesky)/cholesky | solution.py:19
  266.9 0.4 convolution_subtract_fusion.5
  267.3 11.7 %cholesky.255 = f32[128,128]{1,0:T(8,128)S(1)} custom-call(f32[128,128]{1,0:T(8,128)S(1)} %convolution_subtract_fusion.5), custom_call_target="Cholesky" | custom-call | tf_op jit(solution)/shard_map/jit(cholesky)/cholesky | solution.py:19
  279.0 0.7 compare_reduce_fusion
  279.7 0.9 compare_reduce_fusion.2
  283.3 10.3 %while.1 = (s32[]{:T(128)}, f32[512,512]{1,0:T(8,128)S(1)}, s32[4,2]{0,1:T(2,128)S(1)}, f32[4,128,128]{2,1,0:T(8,128)}, s32[]{:T(128)}) while((s32[]{:T(128)}, f32[512,512]{1,0:T(8,128)S(1)}, s32[4,2]{0,1:T(2,128)S(1)}, f32[4,128,128]{2,1,0:T(8,128)}, s32[]{:T(128)}) %tuple.31), condition=%wide.while_cond, body=%wide.while_body.sunk | while | flops 2 | bytes 132705 | solution.py:21
  283.3 0.5 fusion.56
  283.9 2.0 bitcast_dynamic-update-slice_fusion.2
  285.9 0.5 fusion.56
  286.4 2.0 bitcast_dynamic-update-slice_fusion.2
  288.5 0.5 fusion.56
  289.0 2.0 bitcast_dynamic-update-slice_fusion.2
  291.1 0.5 fusion.56
  291.6 2.0 bitcast_dynamic-update-slice_fusion.2
  293.6 40.1 %custom-call.33 = f32[4,128,128]{1,2,0:T(8,128)S(1)} custom-call(f32[4,128,128]{2,1,0:T(8,128)} %get-tuple-element.9), custom_call_target="InvertDiagBlocksLowerTriangular" | custom-call | tf_op jit(solution)/shard_map/triangular_solve | solution.py:21
  333.7 1.2 fusion.20
  334.9 0.4 convolution_subtract_fusion.1
  335.3 0.4 fusion.32
  335.7 0.4 convolution_subtract_fusion
  336.2 0.4 fusion.30
  336.6 0.6 convolution_subtract_fusion.2
  337.3 0.4 fusion.29
  337.7 14.6 %convolution_multiply_fusion = f32[2048,512]{1,0:T(8,128)S(1)} fusion(f32[512,2048]{1,0:T(8,128)S(1)} %copy-done.1, f32[128,512]{1,0:T(8,128)S(1)} %fusion.29, f32[128,512]{1,0:T(8,128)S(1)} %fusion.30, f32[128,512]{1,0:T(8,128)S(1)} %fusion.32, f32[128,512]{1,0:T(8,128)S(1)} %fusion.20), kind=kOutput, calls=%fused_computation.3 | convolution fusion | flops 6444285952 | bytes 9437184 | tf_op jit(solution)/shard_map/dot_general | solution.py:22
  352.3 1.9 copy-done.2
  354.2 6.1 %fusion = f32[512,2048]{1,0:T(8,128)} fusion(bf16[2048,2048]{1,0:T(8,128)(2,1)S(1)} %bitcast.58, f32[2048,512]{1,0:T(8,128)S(1)} %convolution_multiply_fusion), kind=kOutput, calls=%fused_computation.4 | convolution fusion | flops 4296015872 | bytes 16777216 | tf_op jit(solution)/shard_map/dot_general | solution.py:32
  361.0 3.1 dynamic-slice_select_fusion
  364.1 90.6 %reduce-scatter.2.cloned.1.call-done = f32[32,2048]{1,0:T(8,128)} async-done(((f32[512,2048]{1,0:T(8,128)}), f32[32,2048]{1,0:T(8,128)}) %reduce-scatter.2.cloned.1.call-update) | async-done | bytes 262160 | tf_op jit(solution)/shard_map/reduce_scatter | solution.py:31
  454.7 1.7 multiply_select_fusion
  (37 shorter events, 1.7 us)
Async XLA Ops:
  7.2 20.7 %all-gather.3.cloned.1.call-start = ((), (), s32[]{:S(2)}) async-start(), calls=%async_computation.1 | async-start | bytes 6291456 | tf_op jit(solution)/shard_map/all_gather | solution.py:14
  11.3 49.4 %all-gather.5.cloned.1.call-start = ((), (), s32[]{:S(2)}) async-start(), calls=%async_computation.2 | async-start | bytes 25165824 | tf_op jit(solution)/shard_map/all_gather | solution.py:13
  12.1 184.4 %all-reduce.3.cloned.1.call-start = ((), (), s32[]{:S(2)}) async-start(), calls=%async_computation.3 | async-start | bytes 2097152 | tf_op jit(solution)/shard_map/psum | solution.py:18
  73.7 1.9 copy-start
  83.4 371.3 %reduce-scatter.2.cloned.1.call-start = ((), (), s32[]{:S(2)}) async-start(), calls=%async_computation.4 | async-start | bytes 4456448 | tf_op jit(solution)/shard_map/reduce_scatter | solution.py:31
  333.7 4.0 copy-start.1
  336.6 17.6 %slice-start = ((s8[8388608]{0:T(1024)(128)(4,1)}), s8[4194304]{0:T(1024)(128)(4,1)S(1)}, s32[]{:S(2)}) async-start(s8[8388608]{0:T(1024)(128)(4,1)} %bitcast.57), calls=%async_computation.5 | async-start | bytes 8388608
  337.7 16.5 %slice-start.1 = ((s8[8388608]{0:T(1024)(128)(4,1)}), s8[4194304]{0:T(1024)(128)(4,1)S(1)}, s32[]{:S(2)}) async-start(s8[8388608]{0:T(1024)(128)(4,1)} %bitcast.57), calls=%async_computation.6 | async-start | bytes 8388608
  352.3 1.9 copy-start.2
Sparse Core Ops, SparseCore 0:
  11.4 16.3 all-gather.2
  29.4 31.2 all-gather.4
  83.5 112.8 all-reduce.2
  360.4 94.2 reduce-scatter.1
where the time goes:
time: 471 us; the launch traced here: 463 us
  waiting for transfers between devices  252 us (54%)
  other arithmetic  130 us (28%)
  matrix products  47.2 us (10%)
  between operations  17.5 us (4%)
  local copies, waits for them, and re-layouts  15.8 us (3%)
    psum x1, waiting for transfers between devices, on_device(): gram_matrix = lax.psum(local_gram, 'seq')  112 us
    reduce_scatter x1, waiting for transfers between devices, on_device(): lax.psum_scatter(lax.dot_general(rounded, key_rows, contract, preferred_e...  90.6 us
    another operation x14, other arithmetic, on_device(): lower_factor = jnp.linalg.cholesky(gram_matrix)  79 us
    another operation x3, other arithmetic, on_device(): lax.linalg.triangular_solve(lower_factor, identity, left_side=True, lower...  40.3 us
    all_gather x1, waiting for transfers between devices, on_device(): whole_keys = lax.all_gather(key_rows, 'grp', axis=1, tiled=True)  32.8 us
    all_gather x1, waiting for transfers between devices, on_device(): whole_probes = lax.all_gather(probes, 'grp', axis=0, tiled=True)  15.7 us
    dot_general x1, matrix products, on_device(): jnp.dot(sketch, inverse.T, precision=lax.Precision.HIGHEST) * root_tokens  14.6 us
    dot_general x1, matrix products, on_device(): jnp.dot(whole_keys, whole_probes, preferred_element_type=jnp.float32)  13 us
  transfers between devices with their start and end apart: 4, of which 4 were waited for; matrix products, arithmetic and copies ran while one was open for 1% of the time, Pallas kernels for 0%

commit v1 on v0

--- a/solution.py
+++ b/solution.py
@@ -15,7 +15,7 @@
     sketch = jnp.dot(whole_keys, whole_probes, preferred_element_type=jnp.float32)
     contract = (((0,), (0,)), ((), ()))
     local_gram = lax.dot_general(sketch, sketch, contract, precision=lax.Precision.HIGHEST)
-    gram_matrix = lax.psum(local_gram, "seq")
+    gram_matrix = jnp.sum(lax.all_gather(local_gram, "seq"), axis=0)
     lower_factor = jnp.linalg.cholesky(gram_matrix)
     identity = jnp.eye(gram_matrix.shape[0], dtype=jnp.float32)
     inverse = lax.linalg.triangular_solve(lower_factor, identity, left_side=True, lower=True)

time: 471 us -> 562 us (1.19)
  waiting for transfers between devices: 252 us -> 332 us
  other arithmetic: 130 us -> 136 us
    all_gather x0 -> x1, waiting for transfers between devices: none -> 192 us  [on_device(): gram_matrix = jnp.sum(lax.all_gather(local_gram, 'seq'), axis=0)]
    psum x1 -> x0, waiting for transfers between devices: 112 us -> none  [on_device(): gram_matrix = lax.psum(local_gram, 'seq')]
    reduce_sum x0 -> x1, other arithmetic: none -> 7.91 us  [on_device(): gram_matrix = jnp.sum(lax.all_gather(local_gram, 'seq'), axis=0)]
where the time goes in v1:
time: 562 us; the launch traced here: 554 us
  waiting for transfers between devices  332 us (59%)
  other arithmetic  136 us (24%)
  matrix products  52 us (9%)
  between operations  17.5 us (3%)
  local copies, waits for them, and re-layouts  16.2 us (3%)
    all_gather x1, waiting for transfers between devices, on_device(): gram_matrix = jnp.sum(lax.all_gather(local_gram, 'seq'), axis=0)  192 us
    reduce_scatter x1, waiting for transfers between devices, on_device(): lax.psum_scatter(lax.dot_general(rounded, key_rows, contract, preferred_e...  89.7 us
    another operation x14, other arithmetic, on_device(): lower_factor = jnp.linalg.cholesky(gram_matrix)  79 us
    another operation x3, other arithmetic, on_device(): lax.linalg.triangular_solve(lower_factor, identity, left_side=True, lower...  40.3 us
    all_gather x1, waiting for transfers between devices, on_device(): whole_keys = lax.all_gather(key_rows, 'grp', axis=1, tiled=True)  32.8 us
    all_gather x1, waiting for transfers between devices, on_device(): whole_probes = lax.all_gather(probes, 'grp', axis=0, tiled=True)  15.7 us
    dot_general x1, matrix products, on_device(): jnp.dot(sketch, inverse.T, precision=lax.Precision.HIGHEST) * root_tokens  14.6 us
    dot_general x1, matrix products, on_device(): jnp.dot(whole_keys, whole_probes, preferred_element_type=jnp.float32)  13 us
  transfers between devices with their start and end apart: 4, of which 4 were waited for; matrix products, arithmetic and copies ran while one was open for 1% of the time, Pallas kernels for 0%

profile of v1, /device:TPU:0, one launch (start us, length us, event | category | flops | bytes accessed | tf_op | source)
XLA Modules:
  0.0 554.1 jit_solution(5761405247406659829)
XLA Ops:
  7.2 4.1 multiply_convert_fusion
  11.4 0.7 all-gather.7.cloned.1.call-update
  12.1 15.7 %all-gather.5.cloned.1.call-done = bf16[4096,512]{1,0:T(8,128)(2,1)} async-done(((bf16[2048,512]{1,0:T(8,128)(2,1)}), bf16[4096,512]{1,0:T(8,128)(2,1)}) %all-gather.5.cloned.1.call-update) | async-done | bytes 4194320 | tf_op jit(solution)/shard_map/all_gather | solution.py:14
  27.8 32.8 %all-gather.7.cloned.1.call-done = bf16[2048,4096]{1,0:T(8,128)(2,1)} async-done(((bf16[2048,2048]{1,0:T(8,128)(2,1)}), bf16[2048,4096]{1,0:T(8,128)(2,1)}) %all-gather.7.cloned.1.call-update) | async-done | bytes 16777232 | tf_op jit(solution)/shard_map/all_gather | solution.py:13
  60.7 13.0 %fusion.42 = f32[512,2048]{1,0:T(8,128)S(1)} fusion(bf16[4096,512]{1,0:T(8,128)(2,1)} %all-gather.5.cloned.1.call-done, bf16[2048,4096]{1,0:T(8,128)(2,1)} %all-gather.7.cloned.1.call-done), kind=kOutput, calls=%fused_computation.84 | convolution fusion | flops 8589934592 | bytes 25165824 | tf_op jit(solution)/shard_map/dot_general | solution.py:15
  73.7 1.9 copy-done
  75.7 7.9 %fusion.43 = f32[512,512]{1,0:T(8,128)} fusion(f32[512,2048]{1,0:T(8,128)S(1)} %fusion.42), kind=kOutput, calls=%fused_computation.85 | convolution fusion | flops 6442450944 | bytes 5242880 | tf_op jit(solution)/shard_map/dot_general | solution.py:17
  84.0 192.5 %all-gather.9.cloned.1.call-done = f32[8192,512]{1,0:T(8,128)} async-done(((f32[512,512]{1,0:T(8,128)}), f32[8192,512]{1,0:T(8,128)}) %all-gather.9.cloned.1.call-update) | async-done | bytes 16777232 | tf_op jit(solution)/shard_map/all_gather | solution.py:18
  276.5 7.9 %reduce_sum.9 = f32[512,512]{1,0:T(8,128)S(1)} reduce(f32[16,512,512]{2,1,0:T(8,128)} %bitcast.58, f32[]{:T(128)} %constant.153.clone.1), dimensions={0}, to_apply=%region_0.0 | reduce | flops 3932160 | bytes 17825796 | tf_op jit(solution)/shard_map/reduce_sum | solution.py:18
  284.4 0.3 copy.6
  285.0 1.0 copy-done.3
  285.9 11.7 %cholesky.104 = f32[128,128]{1,0:T(8,128)S(1)} custom-call(f32[128,128]{1,0:T(8,128)S(1)} %cholesky.266), custom_call_target="Cholesky" | custom-call | tf_op jit(solution)/shard_map/jit(cholesky)/cholesky | solution.py:19
  297.8 9.8 %custom-call.30 = f32[1,128,128]{1,2,0:T(8,128)S(1)} custom-call(f32[1,128,128]{2,1,0:T(8,128)S(1)} %get-tuple-element.29), custom_call_target="InvertDiagBlocksLowerTriangular" | custom-call | tf_op jit(solution)/shard_map/jit(cholesky)/cholesky | solution.py:19
  307.6 1.2 constant_dynamic-update-slice_fusion.2
  308.9 1.3 convolution_subtract_fusion.3
  310.2 12.1 %cholesky.217 = f32[128,128]{1,0:T(8,128)S(1)} custom-call(f32[128,128]{1,0:T(8,128)S(1)} %cholesky.270), custom_call_target="Cholesky" | custom-call | tf_op jit(solution)/shard_map/jit(cholesky)/cholesky | solution.py:19
  322.3 9.8 %custom-call.31 = f32[1,128,128]{1,2,0:T(8,128)S(1)} custom-call(f32[1,128,128]{2,1,0:T(8,128)S(1)} %get-tuple-element.26), custom_call_target="InvertDiagBlocksLowerTriangular" | custom-call | tf_op jit(solution)/shard_map/jit(cholesky)/cholesky | solution.py:19
  332.4 1.3 convolution_subtract_fusion.4
  333.7 11.7 %cholesky.238 = f32[128,128]{1,0:T(8,128)S(1)} custom-call(f32[128,128]{1,0:T(8,128)S(1)} %cholesky.275), custom_call_target="Cholesky" | custom-call | tf_op jit(solution)/shard_map/jit(cholesky)/cholesky | solution.py:19
  345.4 0.7 compare_reduce_fusion.1
  346.2 9.8 %custom-call.32 = f32[1,128,128]{1,2,0:T(8,128)S(1)} custom-call(f32[1,128,128]{2,1,0:T(8,128)S(1)} %get-tuple-element.23), custom_call_target="InvertDiagBlocksLowerTriangular" | custom-call | tf_op jit(solution)/shard_map/jit(cholesky)/cholesky | solution.py:19
  356.2 1.2 convolution_subtract_fusion.5
  357.4 11.9 %cholesky.255 = f32[128,128]{1,0:T(8,128)S(1)} custom-call(f32[128,128]{1,0:T(8,128)S(1)} %convolution_subtract_fusion.5), custom_call_target="Cholesky" | custom-call | tf_op jit(solution)/shard_map/jit(cholesky)/cholesky | solution.py:19
  369.3 0.6 compare_reduce_fusion
  370.0 0.7 compare_reduce_fusion.2
  373.3 10.9 %while.1 = (s32[]{:T(128)}, f32[512,512]{1,0:T(8,128)S(1)}, s32[4,2]{0,1:T(2,128)S(1)}, f32[4,128,128]{2,1,0:T(8,128)}, s32[]{:T(128)}) while((s32[]{:T(128)}, f32[512,512]{1,0:T(8,128)S(1)}, s32[4,2]{0,1:T(2,128)S(1)}, f32[4,128,128]{2,1,0:T(8,128)}, s32[]{:T(128)}) %tuple.31), condition=%wide.while_cond, body=%wide.while_body.sunk | while | flops 2 | bytes 132705 | solution.py:21
  373.4 0.6 fusion.56
  374.0 2.1 bitcast_dynamic-update-slice_fusion.2
  376.1 0.6 fusion.56
  376.7 2.1 bitcast_dynamic-update-slice_fusion.2
  378.9 0.6 fusion.56
  379.5 2.1 bitcast_dynamic-update-slice_fusion.2
  381.6 0.6 fusion.56
  382.2 2.1 bitcast_dynamic-update-slice_fusion.2
  384.2 40.1 %custom-call.33 = f32[4,128,128]{1,2,0:T(8,128)S(1)} custom-call(f32[4,128,128]{2,1,0:T(8,128)} %get-tuple-element.9), custom_call_target="InvertDiagBlocksLowerTriangular" | custom-call | tf_op jit(solution)/shard_map/triangular_solve | solution.py:21
  424.4 0.3 fusion.20
  424.7 0.4 convolution_subtract_fusion.1
  425.1 0.4 fusion.32
  425.5 0.4 convolution_subtract_fusion
  426.0 1.3 fusion.30
  427.2 0.6 convolution_subtract_fusion.2
  427.9 1.6 fusion.29
  429.5 14.6 %convolution_multiply_fusion = f32[2048,512]{1,0:T(8,128)S(1)} fusion(f32[512,2048]{1,0:T(8,128)S(1)} %copy-done.1, f32[128,512]{1,0:T(8,128)S(1)} %fusion.29, f32[128,512]{1,0:T(8,128)S(1)} %fusion.30, f32[128,512]{1,0:T(8,128)S(1)} %fusion.32, f32[128,512]{1,0:T(8,128)S(1)} %fusion.20), kind=kOutput, calls=%fused_computation.3 | convolution fusion | flops 6444285952 | bytes 9437184 | tf_op jit(solution)/shard_map/dot_general | solution.py:22
  444.1 1.9 copy-done.2
  446.0 6.1 %fusion = f32[512,2048]{1,0:T(8,128)} fusion(bf16[2048,2048]{1,0:T(8,128)(2,1)S(1)} %bitcast.60, f32[2048,512]{1,0:T(8,128)S(1)} %convolution_multiply_fusion), kind=kOutput, calls=%fused_computation.4 | convolution fusion | flops 4296015872 | bytes 16777216 | tf_op jit(solution)/shard_map/dot_general | solution.py:32
  452.8 3.1 dynamic-slice_select_fusion
  455.8 89.7 %reduce-scatter.2.cloned.1.call-done = f32[32,2048]{1,0:T(8,128)} async-done(((f32[512,2048]{1,0:T(8,128)}), f32[32,2048]{1,0:T(8,128)}) %reduce-scatter.2.cloned.1.call-update) | async-done | bytes 262160 | tf_op jit(solution)/shard_map/reduce_scatter | solution.py:31
  545.6 1.7 multiply_select_fusion
  (42 shorter events, 2.0 us)
Async XLA Ops:
  7.2 20.7 %all-gather.5.cloned.1.call-start = ((), (), s32[]{:S(2)}) async-start(), calls=%async_computation.1 | async-start | bytes 6291456 | tf_op jit(solution)/shard_map/all_gather | solution.py:14
  11.3 49.4 %all-gather.7.cloned.1.call-start = ((), (), s32[]{:S(2)}) async-start(), calls=%async_computation.2 | async-start | bytes 25165824 | tf_op jit(solution)/shard_map/all_gather | solution.py:13
  12.1 264.4 %all-gather.9.cloned.1.call-start = ((), (), s32[]{:S(2)}) async-start(), calls=%async_computation.4 | async-start | bytes 17825792 | tf_op jit(solution)/shard_map/all_gather | solution.py:18
  73.7 1.9 copy-start
  83.5 462.0 %reduce-scatter.2.cloned.1.call-start = ((), (), s32[]{:S(2)}) async-start(), calls=%async_computation.3 | async-start | bytes 4456448 | tf_op jit(solution)/shard_map/reduce_scatter | solution.py:31
  285.0 1.0 copy-start.3
  424.4 0.7 copy-start.4
  424.4 5.1 copy-start.1
  427.2 18.8 %slice-start = ((s8[8388608]{0:T(1024)(128)(4,1)}), s8[4194304]{0:T(1024)(128)(4,1)S(1)}, s32[]{:S(2)}) async-start(s8[8388608]{0:T(1024)(128)(4,1)} %bitcast.59), calls=%async_computation.5 | async-start | bytes 8388608
  429.5 16.5 %slice-start.1 = ((s8[8388608]{0:T(1024)(128)(4,1)}), s8[4194304]{0:T(1024)(128)(4,1)S(1)}, s32[]{:S(2)}) async-start(s8[8388608]{0:T(1024)(128)(4,1)} %bitcast.59), calls=%async_computation.6 | async-start | bytes 8388608
  444.1 1.9 copy-start.2
Sparse Core Ops, SparseCore 0:
  11.4 16.3 all-gather.4
  29.4 31.2 all-gather.6
  83.7 192.7 all-gather.8
  452.2 93.3 reduce-scatter.1
